TPU v7x, 32 devices: a whole 2x2x4 slice. The times are simulated.
32 devices in a mesh: dp: 8 (over z, y), tm: 4 (over x, core).
Axes of the slice: x: 2, y: 2, z: 4, core: 2. Of those that a mesh axis runs over, the one named last changes fastest.
Arguments:
- currents: bfloat16 [8, 32, 128, 1280], P('dp', 'tm'), may hold values from -4 to 4, as said below
- mixing: float32 [32, 32], replicated, may hold values from -1 to 1, as said below
- threshold: float32 [32], replicated, may hold values from -4 to 4, as said below
- weight: bfloat16 [1280, 1280], replicated, may hold values from -0.15625 to 0.15625
- bias: float32 [1280], replicated, may hold values from -3 to 3
- cotangent: bfloat16 [8, 32, 128, 1280], P('dp', 'tm'), may hold values from -6 to 6
Outputs:
- output: bfloat16 [8, 32, 128, 1280], P('dp', 'tm')
- current_grad: bfloat16 [8, 32, 128, 1280], P('dp', 'tm')
- weight_grad: bfloat16 [1280, 1280], P(('dp', 'tm'))
- mixing_grad: float32 [32, 32], replicated
- threshold_grad: float32 [32], replicated
- bias_grad: float32 [1280], replicated
Inputs may be any that keep to these rules, and one draw needn't show every extreme that they name: `currents`: every entry is a multiple of 1/16. `mixing`: every entry is a multiple of 1/16. threshold: every entry is an odd multiple of 1/512, so that every membrane value (a multiple of 1/256) lies at least 1/512 from its threshold.
All inputs are finite; a program needn't handle non-finite values.
Results may differ from a plain program's by a relative error of at most 0.0049.
Values may be sent and summed in bfloat16 or wider, within the bound.
No kernel may reach another device: no remote copies, remote signals or barrier semaphores. Data moves between devices by JAX's collectives and lax.ppermute only.
A program may use at most 128 MiB of HBM per device.

v0:
```python
import jax
import jax.numpy as jnp
from jax import lax
from jax.sharding import PartitionSpec as P


def neuron_forward(currents, mixing, threshold):
    highest = lax.Precision.HIGHEST
    wide_cur = currents.astype(jnp.float32)
    membrane = jnp.einsum("tj,ijnd->itnd", mixing, wide_cur, precision=highest)
    shifted = membrane - threshold[None, :, None, None]
    spikes = (shifted > 0).astype(jnp.bfloat16)
    sigmoid_val = jax.nn.sigmoid(shifted)
    surrogate = sigmoid_val * (1.0 - sigmoid_val)
    return (wide_cur, spikes, surrogate)


def neuron_backward(spike_grad, surrogate, mixing, wide_cur):
    highest = lax.Precision.HIGHEST
    membrane_grad = spike_grad.astype(jnp.float32) * surrogate
    input_grad = jnp.einsum("tj,itnd->ijnd", mixing, membrane_grad, precision=highest).astype(
        jnp.bfloat16
    )
    mixing_term = jnp.einsum("itnd,ijnd->tj", membrane_grad, wide_cur, precision=highest)
    threshold_term = -jnp.sum(membrane_grad, axis=(0, 2, 3))
    return (input_grad, mixing_term, threshold_term)


def body(currents, mixing, threshold, weight, bias, cotangent):
    shape = cotangent.shape
    width = shape[3]
    tok_cur = lax.all_to_all(currents, "tm", split_axis=2, concat_axis=1, tiled=True)
    wide_cur, tok_spikes, surrogate = neuron_forward(tok_cur, mixing, threshold)
    spikes = lax.all_to_all(tok_spikes, "tm", split_axis=1, concat_axis=2, tiled=True)
    spike_rows = spikes.reshape(-1, width)
    grad_rows = cotangent.reshape(-1, width)
    output = (
        (jnp.dot(spike_rows, weight, preferred_element_type=jnp.float32) + bias)
        .astype(jnp.bfloat16)
        .reshape(shape)
    )
    spike_grad = (
        jnp.einsum("re,de->rd", grad_rows, weight, preferred_element_type=jnp.float32)
        .astype(jnp.bfloat16)
        .reshape(shape)
    )
    weight_term = jnp.einsum("rd,re->de", spike_rows, grad_rows, preferred_element_type=jnp.float32)
    bias_term = jnp.sum(grad_rows.astype(jnp.float32), axis=0)
    tok_grad = lax.all_to_all(spike_grad, "tm", split_axis=2, concat_axis=1, tiled=True)
    tok_cgrad, mixing_term, threshold_term = neuron_backward(tok_grad, surrogate, mixing, wide_cur)
    current_grad = lax.all_to_all(tok_cgrad, "tm", split_axis=1, concat_axis=2, tiled=True)
    weight_sum = lax.psum_scatter(weight_term, ("dp", "tm"), scatter_dimension=0, tiled=True)
    mixing_grad, threshold_grad, bias_grad = lax.psum(
        (mixing_term, threshold_term, bias_term), ("dp", "tm")
    )
    return (
        output,
        current_grad,
        weight_sum.astype(jnp.bfloat16),
        mixing_grad,
        threshold_grad,
        bias_grad,
    )


def solution(mesh):
    return jax.shard_map(
        body,
        mesh=mesh,
        in_specs=(P("dp", "tm", None, None), P(), P(), P(), P(), P("dp", "tm", None, None)),
        out_specs=(
            P("dp", "tm", None, None),
            P("dp", "tm", None, None),
            P(("dp", "tm"), None),
            P(),
            P(),
            P(),
        ),
        check_vma=False,
    )
```

profile of v0, /device:TPU:0, one launch (start us, length us, event | category | flops | bytes accessed | tf_op | source)
XLA Modules:
  0.0 300.1 jit_solution(4259585015621780677)
XLA Ops:
  7.2 0.0 copy-start
  7.2 1.9 copy-done
  9.1 5.3 %convolution_convert_fusion = bf16[1024,1280]{1,0:T(8,128)(2,1)S(1)} fusion(bf16[1024,1280]{1,0:T(8,128)(2,1)} %bitcast.77, bf16[1280,1280]{1,0:T(8,128)(2,1)S(1)} %copy-done), kind=kOutput, calls=%fused_computation.12 | convolution fusion | flops 3356753920 | bytes 8519680 | tf_op jit(solution)/shard_map/re,de->rd/dot_general | solution.py:43
  14.4 2.9 copy.33
  17.4 4.5 %all-to-all-start.2 = ((bf16[1,8,128,1280]{3,1,0,2:T(8,128)(2,1)}), bf16[1,8,128,1280]{3,1,0,2:T(8,128)(2,1)}, u32[]{:S(2)}, u32[]{:S(2)}) async-start(bf16[1,8,128,1280]{3,1,0,2:T(8,128)(2,1)} %copy.33), calls=%async_computation.2 | async-start | bytes 5242880 | tf_op jit(solution)/shard_map/all_to_all | solution.py:49
  21.9 4.7 %copy.29 = bf16[1,8,128,1280]{3,1,0,2:T(8,128)(2,1)} copy(bf16[1,8,128,1280]{3,2,1,0:T(8,128)(2,1)} %param.6) | data formatting | bytes 5242880 | tf_op args[0]
  26.6 27.3 %all-to-all-done.2 = bf16[1,8,128,1280]{3,1,0,2:T(8,128)(2,1)} async-done(((bf16[1,8,128,1280]{3,1,0,2:T(8,128)(2,1)}), bf16[1,8,128,1280]{3,1,0,2:T(8,128)(2,1)}, u32[]{:S(2)}, u32[]{:S(2)}) %all-to-all-start.2) | async-done | bytes 2621472 | tf_op jit(solution)/shard_map/all_to_all | solution.py:49
  53.9 4.6 %all-to-all-start = ((bf16[1,8,128,1280]{3,1,0,2:T(8,128)(2,1)}), bf16[1,8,128,1280]{3,1,0,2:T(8,128)(2,1)}, u32[]{:S(2)}, u32[]{:S(2)}) async-start(bf16[1,8,128,1280]{3,1,0,2:T(8,128)(2,1)} %copy.29), calls=%async_computation | async-start | bytes 5242880 | tf_op jit(solution)/shard_map/all_to_all | solution.py:32
  58.5 0.0 reduce-scatter.2.cloned.1.call-start
  58.5 2.2 copy.34
  60.7 0.0 copy-start.4
  60.8 0.0 copy-start.5
  60.8 3.0 convert_bitcast_fusion
  63.7 26.1 %all-to-all-done = bf16[1,8,128,1280]{3,1,0,2:T(8,128)(2,1)} async-done(((bf16[1,8,128,1280]{3,1,0,2:T(8,128)(2,1)}), bf16[1,8,128,1280]{3,1,0,2:T(8,128)(2,1)}, u32[]{:S(2)}, u32[]{:S(2)}) %all-to-all-start) | async-done | bytes 2621472 | tf_op jit(solution)/shard_map/all_to_all | solution.py:32
  89.8 0.0 copy-done.4
  89.8 0.0 copy-done.5
  89.8 10.1 %fusion.24 = (f32[32]{0:T(128)S(1)}, f32[1,32,32,1280]{3,1,2,0:T(8,128)}, f32[32,1280,32]{1,2,0:T(8,128)S(1)}) fusion(f32[32]{0:T(128)S(1)} %copy-done.5, f32[1,4,8,32,1280]{4,3,1,2,0:T(8,128)} %convert_bitcast_fusion, f32[32,32]{1,0:T(8,128)S(1)} %copy-done.4, bf16[1,8,4,32,1280]{4,1,3,2,0:T(8,128)(2,1)} %bitcast), kind=kOutput, calls=%fused_computation.23 | convolution fusion | flops 513802208 | bytes 18354432 | tf_op jit(solution)/shard_map/tj,ijnd->itnd/dot_general | solution.py:10
  100.0 0.8 fusion.11
  100.8 1.4 copy.31
  102.2 33.8 %all_to_all.57 = bf16[1,32,32,1280]{3,2,0,1:T(8,128)(2,1)S(1)} all-to-all(bf16[1,32,32,1280]{3,2,0,1:T(8,128)(2,1)S(1)} %copy.31), channel_id=1, replica_groups=mesh['dp'=8,'tm'=4] {'tm'}, dimensions={1} | all-to-all | bytes 5242880 | tf_op jit(solution)/shard_map/all_to_all | solution.py:34
  136.0 0.0 copy-start.1
  136.0 0.2 copy.32
  136.2 0.0 copy-start.2
  136.3 1.5 copy-done.2
  137.7 1.0 copy-done.1
  138.7 5.6 %fusion.26 = f32[1280,1280]{1,0:T(8,128)} fusion(bf16[1024,1280]{1,0:T(8,128)(2,1)S(1)} %bitcast.79, bf16[1024,1280]{1,0:T(8,128)(2,1)S(1)} %bitcast.78), kind=kOutput, calls=%fused_computation.24 | convolution fusion | flops 3355443200 | bytes 11796480 | tf_op jit(solution)/shard_map/rd,re->de/dot_general | solution.py:47
  144.3 0.0 reduce-scatter.2.cloned.1.call-update
  144.3 7.1 %fusion.8 = bf16[1,32,32,1280]{3,1,2,0:T(8,128)(2,1)S(1)} fusion(f32[1,32,32,1280]{3,1,2,0:T(8,128)} %get-tuple-element.10, f32[32,32]{1,0:T(8,128)S(1)} %copy-done.4), kind=kOutput, calls=%fused_computation.13 | convolution fusion | flops 504627200 | bytes 7868416 | tf_op jit(solution)/shard_map/tj,itnd->ijnd/dot_general | solution.py:21
  151.4 2.9 copy.37
  154.3 4.6 %all-to-all-start.3 = ((bf16[1,32,32,1280]{3,2,0,1:T(8,128)(2,1)}), bf16[1,32,32,1280]{3,2,0,1:T(8,128)(2,1)}, u32[]{:S(2)}, u32[]{:S(2)}) async-start(bf16[1,32,32,1280]{3,2,0,1:T(8,128)(2,1)} %copy.37), calls=%async_computation.3 | async-start | bytes 5242880 | tf_op jit(solution)/shard_map/all_to_all | solution.py:51
  158.9 2.2 convert_reduce_fusion
  161.1 5.8 %fusion.17 = f32[32,32]{1,0:T(8,128)S(1)} fusion(bf16[1,8,4,32,1280]{4,1,3,2,0:T(8,128)(2,1)} %bitcast, f32[1,32,32,1280]{3,1,2,0:T(8,128)} %get-tuple-element.10), kind=kOutput, calls=%fused_computation.20 | convolution fusion | flops 503316480 | bytes 7868416 | tf_op jit(solution)/shard_map/itnd,ijnd->tj/dot_general | solution.py:24
  166.9 89.1 %all-reduce = (f32[32,32]{1,0:T(8,128)}, f32[32]{0:T(128)}, f32[1280]{0:T(1024)}) all-reduce(f32[32,32]{1,0:T(8,128)S(1)} %fusion.17, f32[32]{0:T(128)S(1)} %neg.8, f32[1280]{0:T(1024)S(1)} %convert_reduce_fusion), channel_id=1, replica_groups=mesh['dp'=8,'tm'=4] {'dp','tm'}, use_global_device_ids=true, to_apply=%region_1.0 | all-reduce | flops 2336 | bytes 18688 | tf_op jit(solution)/shard_map/psum | solution.py:53
  256.1 0.0 all-to-all-done.3
  256.1 0.0 copy-start.3
  256.1 0.0 copy-start.6
  256.1 3.6 %copy.38 = bf16[1,8,4,32,1280]{4,3,2,1,0:T(8,128)(2,1)} copy(bf16[1,8,4,32,1280]{4,3,1,2,0:T(8,128)(2,1)} %bitcast.21) | data formatting | bytes 5242880 | tf_op jit(solution)/shard_map/all_to_all | solution.py:51
  259.7 0.0 copy-done.3
  259.7 0.0 copy-done.6
  259.7 4.8 %add_convert_fusion = bf16[1024,1280]{1,0:T(8,128)(2,1)} fusion(bf16[1024,1280]{1,0:T(8,128)(2,1)S(1)} %bitcast.80, bf16[1280,1280]{1,0:T(8,128)(2,1)S(1)} %copy-done, f32[1280]{0:T(1024)S(1)} %copy-done.6), kind=kOutput, calls=%fused_computation.9 | convolution fusion | flops 3358064640 | bytes 8524800 | tf_op jit(solution)/shard_map/dot_general | solution.py:38
  264.5 27.2 %reduce-scatter.2.cloned.1.call-done = f32[40,1280]{1,0:T(8,128)} async-done(((f32[1280,1280]{1,0:T(8,128)}), f32[40,1280]{1,0:T(8,128)}) %reduce-scatter.2.cloned.1.call-update) | async-done | bytes 204816 | tf_op jit(solution)/shard_map/reduce_scatter | solution.py:52
  291.7 1.6 convert_element_type.60
  (1 shorter events, 0.0 us)
Async XLA Ops:
  7.2 1.9 copy-start
  17.4 36.5 %all-to-all-start.2 = ((bf16[1,8,128,1280]{3,1,0,2:T(8,128)(2,1)}), bf16[1,8,128,1280]{3,1,0,2:T(8,128)(2,1)}, u32[]{:S(2)}, u32[]{:S(2)}) async-start(bf16[1,8,128,1280]{3,1,0,2:T(8,128)(2,1)} %copy.33), calls=%async_computation.2 | async-start | bytes 5242880 | tf_op jit(solution)/shard_map/all_to_all | solution.py:49
  53.9 35.9 %all-to-all-start = ((bf16[1,8,128,1280]{3,1,0,2:T(8,128)(2,1)}), bf16[1,8,128,1280]{3,1,0,2:T(8,128)(2,1)}, u32[]{:S(2)}, u32[]{:S(2)}) async-start(bf16[1,8,128,1280]{3,1,0,2:T(8,128)(2,1)} %copy.29), calls=%async_computation | async-start | bytes 5242880 | tf_op jit(solution)/shard_map/all_to_all | solution.py:32
  58.5 233.2 %reduce-scatter.2.cloned.1.call-start = ((), (), s32[]{:S(2)}) async-start(), calls=%async_computation.5 | async-start | bytes 6758400 | tf_op jit(solution)/shard_map/reduce_scatter | solution.py:52
  60.7 29.1 %copy-start.4 = (f32[32,32]{1,0:T(8,128)S(1)}, f32[32,32]{1,0:T(8,128)}, u32[]{:S(2)}) copy-start(f32[32,32]{1,0:T(8,128)} %param.7) | copy-start | bytes 12292
  60.8 29.1 %copy-start.5 = (f32[32]{0:T(128)S(1)}, f32[32]{0:T(128)}, u32[]{:S(2)}) copy-start(f32[32]{0:T(128)} %param.8) | copy-start | bytes 388
  136.0 2.7 copy-start.1
  136.2 1.5 copy-start.2
  154.3 101.7 %all-to-all-start.3 = ((bf16[1,32,32,1280]{3,2,0,1:T(8,128)(2,1)}), bf16[1,32,32,1280]{3,2,0,1:T(8,128)(2,1)}, u32[]{:S(2)}, u32[]{:S(2)}) async-start(bf16[1,32,32,1280]{3,2,0,1:T(8,128)(2,1)} %copy.37), calls=%async_computation.3 | async-start | bytes 5242880 | tf_op jit(solution)/shard_map/all_to_all | solution.py:51
  256.1 3.6 %copy-start.3 = (bf16[1,8,4,32,1280]{4,3,2,1,0:T(8,128)(2,1)S(1)}, bf16[1,8,4,32,1280]{4,3,2,1,0:T(8,128)(2,1)}, u32[]{:S(2)}) copy-start(bf16[1,8,4,32,1280]{4,3,2,1,0:T(8,128)(2,1)} %copy-done.2) | copy-start | bytes 7864324
  256.1 3.6 %copy-start.6 = (f32[1280]{0:T(1024)S(1)}, f32[1280]{0:T(1024)}, u32[]{:S(2)}) copy-start(f32[1280]{0:T(1024)} %param.10) | copy-start | bytes 15364
Sparse Core Ops, SparseCore 0:
  144.4 147.2 reduce-scatter.1
where the time goes:
time: 301 us; the launch traced here: 300 us
  blocking collectives  123 us (41%)
  waiting for transfers between devices  80.6 us (27%)
  matrix products  38.7 us (13%)
  local copies, waits for them, and re-layouts  22.4 us (7%)
  between operations  14.2 us (5%)
  starting transfers between devices  13.7 us (5%)
  other arithmetic  7.52 us (2%)
    psum x1, blocking collectives, body(): lax.psum((mixing_term, threshold_term, bias_term), ('dp', 'tm'))  89.1 us
    all_to_all x1, blocking collectives, body(): lax.all_to_all(tok_spikes, 'tm', split_axis=1, concat_axis=2, tiled=True)  33.8 us
    all_to_all x1, waiting for transfers between devices, body(): lax.all_to_all(spike_grad, 'tm', split_axis=2, concat_axis=1, tiled=True)  27.3 us
    reduce_scatter x1, waiting for transfers between devices, body(): lax.psum_scatter(weight_term, ('dp', 'tm'), scatter_dimension=0, tiled=True)  27.2 us
    all_to_all x1, waiting for transfers between devices, body(): lax.all_to_all(currents, 'tm', split_axis=2, concat_axis=1, tiled=True)  26.1 us
    dot_general x1, matrix products, neuron_forward(): membrane = jnp.einsum('tj,ijnd->itnd', mixing, wide_cur, precision=highest)  10.1 us
    unnamed x15, local copies, waits for them, and re-layouts  9.07 us
    dot_general x1, matrix products, neuron_backward(): jnp.einsum('tj,itnd->ijnd', mixing, membrane_grad, precision=highest)  7.08 us
  transfers between devices with their start and end apart: 4, of which 3 were waited for; matrix products, arithmetic and copies ran while one was open for 12% of the time, Pallas kernels for 0%

commit v1 on v0

--- a/solution.py
+++ b/solution.py
@@ -46,7 +46,19 @@
     )
     weight_term = jnp.einsum("rd,re->de", spike_rows, grad_rows, preferred_element_type=jnp.float32)
     bias_term = jnp.sum(grad_rows.astype(jnp.float32), axis=0)
-    tok_grad = lax.all_to_all(spike_grad, "tm", split_axis=2, concat_axis=1, tiled=True)
+    ways, here = (lax.axis_size("tm"), lax.axis_index("tm"))
+    width_2 = spike_grad.shape[2] // ways
+    dims = list(spike_grad.shape)
+    dims[2] = width_2
+    height = dims[1]
+    dims[1] = height * ways
+    full = jnp.zeros(dims, spike_grad.dtype)
+    for mask in range(ways):
+        part = lax.dynamic_slice_in_dim(spike_grad, (here ^ mask) * width_2, width_2, axis=2)
+        if mask:
+            part = lax.ppermute(part, "tm", [(d, d ^ mask) for d in range(ways)])
+        full = lax.dynamic_update_slice_in_dim(full, part, (here ^ mask) * height, axis=1)
+    tok_grad = full
     tok_cgrad, mixing_term, threshold_term = neuron_backward(tok_grad, surrogate, mixing, wide_cur)
     current_grad = lax.all_to_all(tok_cgrad, "tm", split_axis=1, concat_axis=2, tiled=True)
     weight_sum = lax.psum_scatter(weight_term, ("dp", "tm"), scatter_dimension=0, tiled=True)

time: 301 us -> 288 us (0.957)
  waiting for transfers between devices: 80.6 us -> 63.3 us
  local copies, waits for them, and re-layouts: 22.4 us -> 30.7 us
    ppermute x0 -> x3, waiting for transfers between devices: none -> 36.1 us  [body(): part = lax.ppermute(part, 'tm', [(d, d ^ mask) for d in range(ways)])]
    all_to_all x1 -> x0, waiting for transfers between devices: 27.3 us -> none  [body(): lax.all_to_all(spike_grad, 'tm', split_axis=2, concat_axis=1, tiled=True)]
    all_to_all x1, waiting for transfers between devices: 26.1 us -> 0.01 us  [body(): lax.all_to_all(currents, 'tm', split_axis=2, concat_axis=1, tiled=True)]
    dynamic_update_slice x0 -> x4, local copies, waits for them, and re-layouts: none -> 7.1 us  [body(): lax.dynamic_update_slice_in_dim(full, part, (here ^ mask) * height, axis=1)]
    all_to_all x1 -> x0, starting transfers between devices: 4.55 us -> none  [body(): lax.all_to_all(spike_grad, 'tm', split_axis=2, concat_axis=1, tiled=True)]
    ppermute x0 -> x3, starting transfers between devices: none -> 3.06 us  [body(): part = lax.ppermute(part, 'tm', [(d, d ^ mask) for d in range(ways)])]
    unnamed x15 -> x20, local copies, waits for them, and re-layouts: 9.07 us -> 10.9 us
  transfers between devices with their start and end apart: 4 -> 6, of which waited for: 3 -> 3; matrix products, arithmetic and copies ran while one was open for 12% -> 17% of each run, Pallas kernels for 0% -> 0%
where the time goes in v1:
time: 288 us; the launch traced here: 287 us
  blocking collectives  123 us (43%)
  waiting for transfers between devices  63.3 us (22%)
  matrix products  38.8 us (13%)
  local copies, waits for them, and re-layouts  30.7 us (11%)
  between operations  14.1 us (5%)
  starting transfers between devices  12.2 us (4%)
  other arithmetic  4.57 us (2%)
    psum x1, blocking collectives, body(): lax.psum((mixing_term, threshold_term, bias_term), ('dp', 'tm'))  89.6 us
    ppermute x3, waiting for transfers between devices, body(): part = lax.ppermute(part, 'tm', [(d, d ^ mask) for d in range(ways)])  36.1 us
    all_to_all x1, blocking collectives, body(): lax.all_to_all(tok_spikes, 'tm', split_axis=1, concat_axis=2, tiled=True)  33.8 us
    reduce_scatter x1, waiting for transfers between devices, body(): lax.psum_scatter(weight_term, ('dp', 'tm'), scatter_dimension=0, tiled=True)  27.2 us
    unnamed x20, local copies, waits for them, and re-layouts  10.9 us
    dot_general x1, matrix products, neuron_forward(): membrane = jnp.einsum('tj,ijnd->itnd', mixing, wide_cur, precision=highest)  8.71 us
    dynamic_update_slice x4, local copies, waits for them, and re-layouts, body(): lax.dynamic_update_slice_in_dim(full, part, (here ^ mask) * height, axis=1)  7.1 us
    dot_general x1, matrix products, neuron_backward(): jnp.einsum('tj,itnd->ijnd', mixing, membrane_grad, precision=highest)  7.08 us
  transfers between devices with their start and end apart: 6, of which 3 were waited for; matrix products, arithmetic and copies ran while one was open for 17% of the time, Pallas kernels for 0%

profile of v1, /device:TPU:0, one launch (start us, length us, event | category | flops | bytes accessed | tf_op | source)
XLA Modules:
  0.0 287.1 jit_solution(11610301422428854933)
XLA Ops:
  7.2 0.0 copy-start
  7.2 4.8 %copy.33 = bf16[1,8,128,1280]{3,1,0,2:T(8,128)(2,1)} copy(bf16[1,8,128,1280]{3,2,1,0:T(8,128)(2,1)} %param.6) | data formatting | bytes 5242880 | tf_op args[0]
  12.0 4.6 %all-to-all-start = ((bf16[1,8,128,1280]{3,1,0,2:T(8,128)(2,1)}), bf16[1,8,128,1280]{3,1,0,2:T(8,128)(2,1)}, u32[]{:S(2)}, u32[]{:S(2)}) async-start(bf16[1,8,128,1280]{3,1,0,2:T(8,128)(2,1)} %copy.33), calls=%async_computation | async-start | bytes 5242880 | tf_op jit(solution)/shard_map/all_to_all | solution.py:32
  16.6 0.0 reduce-scatter.2.cloned.1.call-start
  16.6 0.0 copy-done
  16.6 6.8 %convolution_convert_fusion = bf16[1024,1280]{1,0:T(8,128)(2,1)} fusion(bf16[1024,1280]{1,0:T(8,128)(2,1)} %bitcast.69, bf16[1280,1280]{1,0:T(8,128)(2,1)S(1)} %copy-done), kind=kOutput, calls=%fused_computation.11 | convolution fusion | flops 3356753920 | bytes 8519680 | tf_op jit(solution)/shard_map/re,de->rd/dot_general | solution.py:43
  23.4 2.7 constant_dynamic-slice_fusion
  26.1 1.2 copy.47
  27.3 0.5 collective-permute-start
  27.8 1.2 copy.48
  29.0 2.5 collective-permute-start.1
  31.5 1.2 copy.49
  32.7 0.1 collective-permute-start.2
  32.8 0.0 copy-start.1
  32.8 1.8 broadcast_in_dim.2
  34.6 0.0 copy-done.1
  34.6 0.0 copy-start.5
  34.6 0.0 copy-start.6
  34.6 1.2 copy_dynamic-update-slice_fusion
  35.8 0.0 collective-permute-done
  35.8 2.0 constant_dynamic-update-slice_fusion.2
  37.8 25.7 %collective-permute-done.1 = bf16[1,8,32,1280]{3,1,2,0:T(8,128)(2,1)} collective-permute-done((bf16[1,8,32,1280]{3,1,2,0:T(8,128)(2,1)}, bf16[1,8,32,1280]{3,1,2,0:T(8,128)(2,1)}, u32[]{:S(2)}, u32[]{:S(2)}) %collective-permute-start.1) | collective-permute-done | bytes 655392 | tf_op jit(solution)/shard_map/ppermute | solution.py:59
  63.4 2.0 constant_dynamic-update-slice_fusion.1
  65.4 10.4 %collective-permute-done.2 = bf16[1,8,32,1280]{3,1,2,0:T(8,128)(2,1)} collective-permute-done((bf16[1,8,32,1280]{3,1,2,0:T(8,128)(2,1)}, bf16[1,8,32,1280]{3,1,2,0:T(8,128)(2,1)}, u32[]{:S(2)}, u32[]{:S(2)}) %collective-permute-start.2) | collective-permute-done | bytes 655392 | tf_op jit(solution)/shard_map/ppermute | solution.py:59
  75.8 2.0 constant_dynamic-update-slice_fusion
  77.8 0.0 all-to-all-done
  77.8 0.0 copy-done.5
  77.8 0.0 copy-done.6
  77.8 8.7 %fusion.24 = (f32[32]{0:T(128)S(1)}, f32[1,32,32,1280]{3,1,2,0:T(8,128)}, f32[32,1280,32]{1,2,0:T(8,128)S(1)}) fusion(f32[32]{0:T(128)S(1)} %copy-done.6, bf16[1,32,32,1280]{3,1,2,0:T(8,128)(2,1)} %constant_dynamic-update-slice_fusion, f32[32,32]{1,0:T(8,128)S(1)} %copy-done.5, bf16[1,8,4,32,1280]{4,1,3,2,0:T(8,128)(2,1)} %bitcast), kind=kOutput, calls=%fused_computation.30 | convolution fusion | flops 515112928 | bytes 15732992 | tf_op jit(solution)/shard_map/tj,ijnd->itnd/dot_general | solution.py:10
  86.5 0.8 fusion.11
  87.3 1.4 copy.35
  88.7 33.8 %all_to_all.48 = bf16[1,32,32,1280]{3,2,0,1:T(8,128)(2,1)S(1)} all-to-all(bf16[1,32,32,1280]{3,2,0,1:T(8,128)(2,1)S(1)} %copy.35), channel_id=1, replica_groups=mesh['dp'=8,'tm'=4] {'tm'}, dimensions={1} | all-to-all | bytes 5242880 | tf_op jit(solution)/shard_map/all_to_all | solution.py:34
  122.5 0.0 copy-start.2
  122.5 0.2 copy.36
  122.8 0.0 copy-start.3
  122.8 1.5 copy-done.3
  124.2 1.0 copy-done.2
  125.2 5.6 %fusion.26 = f32[1280,1280]{1,0:T(8,128)} fusion(bf16[1024,1280]{1,0:T(8,128)(2,1)S(1)} %bitcast.72, bf16[1024,1280]{1,0:T(8,128)(2,1)S(1)} %bitcast.70), kind=kOutput, calls=%fused_computation.31 | convolution fusion | flops 3355443200 | bytes 11796480 | tf_op jit(solution)/shard_map/rd,re->de/dot_general | solution.py:47
  130.8 0.0 reduce-scatter.2.cloned.1.call-update
  130.8 7.1 %fusion.8 = bf16[1,32,32,1280]{3,1,2,0:T(8,128)(2,1)S(1)} fusion(f32[1,32,32,1280]{3,1,2,0:T(8,128)} %get-tuple-element.10, f32[32,32]{1,0:T(8,128)S(1)} %copy-done.5), kind=kOutput, calls=%fused_computation.12 | convolution fusion | flops 504627200 | bytes 7868416 | tf_op jit(solution)/shard_map/tj,itnd->ijnd/dot_general | solution.py:21
  137.9 2.9 %copy.42 = bf16[1,32,32,1280]{3,2,0,1:T(8,128)(2,1)} copy(bf16[1,32,32,1280]{3,1,2,0:T(8,128)(2,1)S(1)} %fusion.8) | data formatting | bytes 5242880 | tf_op jit(solution)/shard_map/convert_element_type | solution.py:21
  140.9 4.6 %all-to-all-start.2 = ((bf16[1,32,32,1280]{3,2,0,1:T(8,128)(2,1)}), bf16[1,32,32,1280]{3,2,0,1:T(8,128)(2,1)}, u32[]{:S(2)}, u32[]{:S(2)}) async-start(bf16[1,32,32,1280]{3,2,0,1:T(8,128)(2,1)} %copy.42), calls=%async_computation.2 | async-start | bytes 5242880 | tf_op jit(solution)/shard_map/all_to_all | solution.py:63
  145.4 2.2 convert_reduce_fusion
  147.6 5.8 %fusion.17 = f32[32,32]{1,0:T(8,128)S(1)} fusion(bf16[1,8,4,32,1280]{4,1,3,2,0:T(8,128)(2,1)} %bitcast, f32[1,32,32,1280]{3,1,2,0:T(8,128)} %get-tuple-element.10), kind=kOutput, calls=%fused_computation.19 | convolution fusion | flops 503316480 | bytes 7868416 | tf_op jit(solution)/shard_map/itnd,ijnd->tj/dot_general | solution.py:24
  153.5 89.6 %all-reduce = (f32[32,32]{1,0:T(8,128)}, f32[32]{0:T(128)}, f32[1280]{0:T(1024)}) all-reduce(f32[32,32]{1,0:T(8,128)S(1)} %fusion.17, f32[32]{0:T(128)S(1)} %neg.8, f32[1280]{0:T(1024)S(1)} %convert_reduce_fusion), channel_id=1, replica_groups=mesh['dp'=8,'tm'=4] {'dp','tm'}, use_global_device_ids=true, to_apply=%region_1.0 | all-reduce | flops 2336 | bytes 18688 | tf_op jit(solution)/shard_map/psum | solution.py:65
  243.0 0.0 all-to-all-done.2
  243.0 0.0 copy-start.4
  243.0 0.0 copy-start.7
  243.0 3.6 %copy.43 = bf16[1,8,4,32,1280]{4,3,2,1,0:T(8,128)(2,1)} copy(bf16[1,8,4,32,1280]{4,3,1,2,0:T(8,128)(2,1)} %bitcast.18) | data formatting | bytes 5242880 | tf_op jit(solution)/shard_map/all_to_all | solution.py:63
  246.7 0.0 copy-done.4
  246.7 0.0 copy-done.7
  246.7 4.8 %add_convert_fusion = bf16[1024,1280]{1,0:T(8,128)(2,1)} fusion(bf16[1024,1280]{1,0:T(8,128)(2,1)S(1)} %bitcast.73, bf16[1280,1280]{1,0:T(8,128)(2,1)S(1)} %copy-done, f32[1280]{0:T(1024)S(1)} %copy-done.7), kind=kOutput, calls=%fused_computation.8 | convolution fusion | flops 3358064640 | bytes 8524800 | tf_op jit(solution)/shard_map/dot_general | solution.py:38
  251.5 27.2 %reduce-scatter.2.cloned.1.call-done = f32[40,1280]{1,0:T(8,128)} async-done(((f32[1280,1280]{1,0:T(8,128)}), f32[40,1280]{1,0:T(8,128)}) %reduce-scatter.2.cloned.1.call-update) | async-done | bytes 204816 | tf_op jit(solution)/shard_map/reduce_scatter | solution.py:64
  278.7 1.6 convert_element_type.40
  (1 shorter events, 0.0 us)
Async XLA Ops:
  7.2 9.4 %copy-start = (bf16[1280,1280]{1,0:T(8,128)(2,1)S(1)}, bf16[1280,1280]{1,0:T(8,128)(2,1)}, u32[]{:S(2)}) copy-start(bf16[1280,1280]{1,0:T(8,128)(2,1)} %param.9) | copy-start | bytes 9830404
  12.0 65.8 %all-to-all-start = ((bf16[1,8,128,1280]{3,1,0,2:T(8,128)(2,1)}), bf16[1,8,128,1280]{3,1,0,2:T(8,128)(2,1)}, u32[]{:S(2)}, u32[]{:S(2)}) async-start(bf16[1,8,128,1280]{3,1,0,2:T(8,128)(2,1)} %copy.33), calls=%async_computation | async-start | bytes 5242880 | tf_op jit(solution)/shard_map/all_to_all | solution.py:32
  16.6 262.1 %reduce-scatter.2.cloned.1.call-start = ((), (), s32[]{:S(2)}) async-start(), calls=%async_computation.4 | async-start | bytes 6758400 | tf_op jit(solution)/shard_map/reduce_scatter | solution.py:64
  27.3 8.5 %collective-permute-start = (bf16[1,8,32,1280]{3,1,2,0:T(8,128)(2,1)}, bf16[1,8,32,1280]{3,1,2,0:T(8,128)(2,1)}, u32[]{:S(2)}, u32[]{:S(2)}) collective-permute-start(bf16[1,8,32,1280]{3,1,2,0:T(8,128)(2,1)} %copy.47), channel_id=1, source_target_pairs={{0,1},{1,0},{2,3},{3,2},{4,5},{5,4},{6,7},{7,6},{8,9},{9,8},{10,11... | collective-permute-start | bytes 1966088 | tf_op jit(solution)/shard_map/ppermute | solution.py:59
  29.0 34.4 %collective-permute-start.1 = (bf16[1,8,32,1280]{3,1,2,0:T(8,128)(2,1)}, bf16[1,8,32,1280]{3,1,2,0:T(8,128)(2,1)}, u32[]{:S(2)}, u32[]{:S(2)}) collective-permute-start(bf16[1,8,32,1280]{3,1,2,0:T(8,128)(2,1)} %copy.48), channel_id=1, source_target_pairs={{0,2},{1,3},{2,0},{3,1},{4,6},{5,7},{6,4},{7,5},{8,10},{9,11},{10,... | collective-permute-start | bytes 1966088 | tf_op jit(solution)/shard_map/ppermute | solution.py:59
  32.7 43.1 %collective-permute-start.2 = (bf16[1,8,32,1280]{3,1,2,0:T(8,128)(2,1)}, bf16[1,8,32,1280]{3,1,2,0:T(8,128)(2,1)}, u32[]{:S(2)}, u32[]{:S(2)}) collective-permute-start(bf16[1,8,32,1280]{3,1,2,0:T(8,128)(2,1)} %copy.49), channel_id=1, source_target_pairs={{0,3},{1,2},{2,1},{3,0},{4,7},{5,6},{6,5},{7,4},{8,11},{9,10},{10,... | collective-permute-start | bytes 1966088 | tf_op jit(solution)/shard_map/ppermute | solution.py:59
  32.8 1.8 copy-start.1
  34.6 43.2 %copy-start.5 = (f32[32,32]{1,0:T(8,128)S(1)}, f32[32,32]{1,0:T(8,128)}, u32[]{:S(2)}) copy-start(f32[32,32]{1,0:T(8,128)} %param.7) | copy-start | bytes 12292
  34.6 43.2 %copy-start.6 = (f32[32]{0:T(128)S(1)}, f32[32]{0:T(128)}, u32[]{:S(2)}) copy-start(f32[32]{0:T(128)} %param.8) | copy-start | bytes 388
  122.5 2.7 copy-start.2
  122.8 1.5 copy-start.3
  140.9 102.2 %all-to-all-start.2 = ((bf16[1,32,32,1280]{3,2,0,1:T(8,128)(2,1)}), bf16[1,32,32,1280]{3,2,0,1:T(8,128)(2,1)}, u32[]{:S(2)}, u32[]{:S(2)}) async-start(bf16[1,32,32,1280]{3,2,0,1:T(8,128)(2,1)} %copy.42), calls=%async_computation.2 | async-start | bytes 5242880 | tf_op jit(solution)/shard_map/all_to_all | solution.py:63
  243.0 3.6 %copy-start.4 = (bf16[1,8,4,32,1280]{4,3,2,1,0:T(8,128)(2,1)S(1)}, bf16[1,8,4,32,1280]{4,3,2,1,0:T(8,128)(2,1)}, u32[]{:S(2)}) copy-start(bf16[1,8,4,32,1280]{4,3,2,1,0:T(8,128)(2,1)} %copy-done.3) | copy-start | bytes 7864324
  243.0 3.6 %copy-start.7 = (f32[1280]{0:T(1024)S(1)}, f32[1280]{0:T(1024)}, u32[]{:S(2)}) copy-start(f32[1280]{0:T(1024)} %param.10) | copy-start | bytes 15364
Sparse Core Ops, SparseCore 0:
  131.0 147.6 reduce-scatter.1
